TPU v7x, 128 devices: a whole 4x4x4 slice. The times are simulated.
128 devices in a mesh: sky: 32 (over y, z, core), band: 4 (over x).
Axes of the slice: x: 4, y: 4, z: 4, core: 2. Of those that a mesh axis runs over, the one named last changes fastest.
Arguments:
- exposures: bfloat16 [32, 4, 1024, 1024], P('sky', 'band'), may hold values from -6 to 6
- inv_variance: bfloat16 [32, 4, 1024, 1024], P('sky', 'band'), may hold values from 0.25 to 4
- mask_planes: int32 [32, 4, 2, 35], P('sky', 'band'), may hold values from 0 to 1073741823, as said below
- sky_columns: int32 [32, 4, 8], replicated, may hold values from 0 to 31, as said below
- basis_rows: float32 [9, 25], replicated, may hold values from -1 to 1
- basis_cols: float32 [9, 25], replicated, may hold values from -1 to 1
- match_coeffs: float32 [32, 4, 9], P('sky', 'band'), may hold values from -2 to 2
- detect_taps: float32 [4, 31], P('band'), may hold values from 0.05 to 0.3
Outputs:
- difference: bfloat16 [32, 4, 1024, 1024], P('sky', 'band')
- detection: float32 [1024, 4096], P('band', 'sky')
Inputs may be any that keep to these rules, and one draw needn't show every extreme that they name: Each row sky_columns[e, b] holds 8 consecutive sky tile columns in order, counted modulo 32; every sky tile column is covered by some exposure of every band. Bit j of mask_planes[e, b, 0, w] marks pixel column 30 w + j of that exposure as bad and bit j of mask_planes[e, b, 1, w] pixel row 30 w + j; bits past 1024 are ignored. In every draw some word has all 30 bits set.
All inputs are finite; a program needn't handle non-finite values.
Results may differ from a plain program's by a relative error of at most 0.0095.
Values may be sent and summed in bfloat16 or wider, within the bound.
A program may use at most 128 MiB of HBM per device.

v0:
```python
import jax
import jax.numpy as jnp
from jax import lax
from jax.sharding import PartitionSpec as P

TILE = 128
NB = 9
TAPS = 25
DTAPS = 31


def with_halo(block, sides, width):
    for axis, dim in sides:
        count = lax.axis_size(axis)
        forward = [(i, i + 1) for i in range(count - 1)]
        forward.append((count - 1, 0))
        backward = [(target, source) for source, target in forward]
        low = lax.ppermute(
            lax.slice_in_dim(block, block.shape[dim] - width, None, axis=dim), axis, forward
        )
        high = lax.ppermute(lax.slice_in_dim(block, 0, width, axis=dim), axis, backward)
        block = jnp.concatenate([low, block, high], axis=dim)
    return block


def cut_along(value, dim, length):
    dims = value.shape
    pieces = value.reshape(*dims[:dim], length, dims[dim] // length, *dims[dim + 1 :])
    return jnp.moveaxis(pieces, dim, 0)


def sum_at_owner(value, axis, dim):
    pieces = cut_along(value, dim, lax.axis_size(axis))
    arrived = lax.all_to_all(pieces, axis, split_axis=0, concat_axis=0, tiled=True)
    return arrived.sum(axis=0)


def band_matrix(tap_rows, window_width):
    offsets = (
        jnp.arange(window_width, dtype=jnp.int32)[:, None]
        - jnp.arange(TILE, dtype=jnp.int32)[None, :]
    )
    selector = (
        offsets[:, :, None] == jnp.arange(tap_rows.shape[1], dtype=jnp.int32)[None, None, :]
    ).astype(jnp.float32)
    return jnp.einsum(
        "wtl,kl->kwt", selector, tap_rows.astype(jnp.float32), precision=lax.Precision.HIGHEST
    ).astype(jnp.bfloat16)


def keep_pixels(planes, side_length):
    places = jnp.arange(side_length, dtype=jnp.int32)
    column_bits = jnp.bitwise_and(jnp.right_shift(planes[0][places // 30], places % 30), 1)
    row_bits = jnp.bitwise_and(jnp.right_shift(planes[1][places // 30], places % 30), 1)
    return jnp.logical_and(row_bits[:, None] == 0, column_bits[None, :] == 0)


def psf_match(picture, column_taps, row_taps):
    side_length = picture.shape[1]
    block_count = side_length // TILE
    margin = TAPS // 2
    width_full = TILE + 2 * margin
    padded = jnp.pad(picture, ((0, 0), (margin, margin)))
    blocks = jnp.stack(
        [
            padded[:, TILE * block_index : TILE * block_index + width_full]
            for block_index in range(block_count)
        ],
        0,
    )
    column_band = band_matrix(column_taps, width_full)
    column_pass = jnp.einsum(
        "jyw,kwt->kyjt", blocks, column_band, preferred_element_type=jnp.float32
    )
    column_pass = column_pass.reshape(NB, side_length, side_length).astype(jnp.bfloat16)
    row_padded = jnp.pad(column_pass, ((0, 0), (margin, margin), (0, 0)))
    row_blocks = jnp.stack(
        [
            row_padded[:, TILE * block_index : TILE * block_index + width_full, :]
            for block_index in range(block_count)
        ],
        0,
    )
    row_band = band_matrix(row_taps, width_full)
    summed = jnp.einsum("ikwx,kwt->itx", row_blocks, row_band, preferred_element_type=jnp.float32)
    return summed.reshape(side_length, side_length).astype(jnp.bfloat16)


def average_pieces(pieces):
    matched_in, weight_in = pieces
    weight_float = weight_in.astype(jnp.float32)
    numer = jnp.sum(weight_float * matched_in.astype(jnp.float32), axis=1)
    denom = jnp.sum(weight_float, axis=1)
    return (numer / jnp.maximum(denom, 1.0)).astype(jnp.bfloat16)


def subtract_template(template, matched, own_columns, side_length, sky_count):
    gathered = lax.all_gather(template, "sky", axis=1, tiled=True).reshape(
        side_length, sky_count, TILE
    )
    picked = jnp.take(gathered, own_columns, axis=1).reshape(side_length, side_length)
    return (matched.astype(jnp.float32) - picked.astype(jnp.float32)).astype(jnp.bfloat16)


def body(
    exposures,
    inv_variance,
    mask_planes,
    sky_columns,
    basis_rows,
    basis_cols,
    match_coeffs,
    detect_taps,
):
    picture = exposures[0, 0]
    side_length = picture.shape[0]
    block_count = side_length // TILE
    sky_count = lax.axis_size("sky")
    own_sky = lax.axis_index("sky")
    own_band = lax.axis_index("band")
    column_taps = (match_coeffs[0, 0][:, None] * basis_cols).astype(jnp.bfloat16)
    matched = psf_match(picture, column_taps, basis_rows.astype(jnp.bfloat16))
    keep = keep_pixels(mask_planes[0, 0], side_length)
    variance_inv = inv_variance[0, 0]
    weight = jnp.where(keep, variance_inv, jnp.zeros_like(variance_inv))
    own_columns = sky_columns[own_sky, own_band]
    empty_slots = jnp.zeros((side_length, sky_count, TILE), jnp.bfloat16)
    send_matched = empty_slots.at[:, own_columns, :].set(
        matched.reshape(side_length, block_count, TILE)
    )
    send_weight = empty_slots.at[:, own_columns, :].set(
        weight.reshape(side_length, block_count, TILE)
    )
    template = average_pieces(
        (
            lax.all_to_all(send_matched, "sky", split_axis=1, concat_axis=1, tiled=True),
            lax.all_to_all(send_weight, "sky", split_axis=1, concat_axis=1, tiled=True),
        )
    )
    difference = subtract_template(template, matched, own_columns, side_length, sky_count)
    margin = DTAPS // 2
    width_full = TILE + 2 * margin
    filter_band = band_matrix(detect_taps.astype(jnp.bfloat16), width_full)[0]
    widened = with_halo(template, (("sky", 1),), margin)
    smoothed = jnp.dot(widened, filter_band, preferred_element_type=jnp.float32).astype(
        jnp.bfloat16
    )
    smooth_padded = jnp.pad(smoothed, ((margin, margin), (0, 0)))
    smooth_blocks = jnp.stack(
        [
            smooth_padded[TILE * block_index : TILE * block_index + width_full]
            for block_index in range(block_count)
        ],
        0,
    )
    filtered = jnp.einsum(
        "iwx,wt->itx", smooth_blocks, filter_band, preferred_element_type=jnp.float32
    ).reshape(side_length, TILE)
    power = filtered * filtered
    detection = sum_at_owner(power, "band", 0)
    return (difference[None, None], detection)


def solution(mesh):
    in_specs = (
        P("sky", "band", None, None),
        P("sky", "band", None, None),
        P("sky", "band", None, None),
        P(),
        P(),
        P(),
        P("sky", "band", None),
        P("band", None),
    )
    out_specs = (P("sky", "band", None, None), P("band", "sky"))
    return jax.shard_map(body, mesh=mesh, in_specs=in_specs, out_specs=out_specs, check_vma=False)
```

profile of v0, /device:TPU:1, one launch (start us, length us, event | category | flops | bytes accessed | tf_op | source)
XLA Modules:
  0.0 444.7 jit_solution(8928743750772134446)
XLA Ops:
  7.2 2.9 copy.63
  11.6 9.2 %convolution_convert_fusion = bf16[9,128,8,1024]{3,1,2,0:T(8,128)(2,1)} fusion(bf16[8,1024,152]{1,2,0:T(8,128)(2,1)S(1)} %fusion.34, bf16[9,152,128,1]{2,0,1,3:T(8,128)(2,1)S(1)} %fusion.19), kind=kOutput, calls=%fused_computation.8 | convolution fusion | flops 2878341120 | bytes 21714944 | tf_op jit(solution)/shard_map/jyw,kwt->kyjt/dot_general | solution.py:72
  20.8 24.6 %copy.65 = bf16[9,1024,1024]{2,1,0:T(8,128)(2,1)} copy(bf16[9,1024,1024]{1,2,0:T(8,128)(2,1)} %bitcast.238) | data formatting | bytes 37748736 | tf_op jit(solution)/shard_map/convert_element_type | solution.py:75
  45.4 4.3 fusion.2
  49.8 3.8 copy-done.2
  53.6 2.5 fusion.10
  56.1 2.4 fusion.9
  58.5 2.5 fusion.8
  61.0 2.5 fusion.7
  63.5 2.4 fusion.6
  65.9 2.4 fusion.5
  68.4 2.4 fusion.4
  71.4 9.9 %bitcast_convert_fusion = bf16[128,8,1024]{2,0,1:T(8,128)(2,1)S(1)} fusion(bf16[8,9,152,1024]{3,2,1,0:T(8,128)(2,1)} %fusion.4, bf16[9,152,128]{2,0,1:T(8,128)(2,1)S(1)} %fusion.20), kind=kOutput, calls=%fused_computation.9 | convolution fusion | flops 2869952512 | bytes 24860672 | tf_op jit(solution)/shard_map/ikwx,kwt->itx/dot_general | solution.py:85
  81.3 0.6 copy.87
  81.9 1.7 copy.103
  83.8 5.1 %broadcast_in_dim.18.clone.1 = bf16[1024,32,128]{2,0,1:T(8,128)(2,1)} broadcast(bf16[]{:T(256)} %constant.31.clone.1), dimensions={} | broadcast | bytes 8388610 | tf_op jit(solution)/shard_map/broadcast_in_dim | solution.py:127
  88.9 5.7 %scatter_fusion.1 = bf16[1024,32,128]{2,0,1:T(8,128)(2,1)} fusion(bf16[1024,32,128]{2,0,1:T(8,128)(2,1)} %broadcast_in_dim.18.clone.1, s32[8]{0:T(128)S(1)} %fusion.61, bf16[8,1024,128]{2,1,0:T(8,128)(2,1)} %bitcast.250), kind=kCustom, calls=%fused_computation.2 | custom fusion | bytes 6291488 | tf_op jit(solution)/shard_map/scatter | solution.py:128
  94.6 9.6 %all-to-all-start.1 = ((bf16[1024,32,128]{2,0,1:T(8,128)(2,1)}), bf16[1024,32,128]{2,0,1:T(8,128)(2,1)}, u32[]{:S(2)}, u32[]{:S(2)}) async-start(bf16[1024,32,128]{2,0,1:T(8,128)(2,1)} %scatter_fusion.1), calls=%async_computation.1 | async-start | bytes 16777216 | tf_op jit(solution)/shard_map/all_to_all | solution.py:136
  104.3 2.2 copy.86
  107.7 0.7 fusion.67
  108.4 0.7 fusion.64
  109.1 4.5 %compare_select_fusion.2 = s32[1024,1]{0,1:T(1,128)S(1)} fusion(s32[]{:T(128)} %bitcast.97, s32[]{:T(128)} %bitcast.98, s32[]{:T(128)} %bitcast.99, s32[]{:T(128)} %bitcast.100, s32[]{:T(128)} %bitcast.101, s32[]{:T(128)} %bitcast.103, s32[]{:T(128)} %bitcast.102), kind=kLoop, calls=%fused_computation.125 | loop fusion | flops 23552 | bytes 4124 | tf_op jit(solution)/shard_map/gather | solution.py:53
  113.6 0.7 fusion.65
  114.3 0.7 fusion.66
  115.0 4.4 compare_select_fusion.1
  119.5 17.3 %fusion.49 = pred[8,128]{1,0:T(8,128)(4,1)S(1)} fusion(pred[1024]{0:T(1024)(128)(4,1)S(1)} %compare_reduce_fusion, pred[1024]{0:T(1024)(128)(4,1)S(1)} %compare_reduce_fusion.1, pred[1024]{0:T(1024)(128)(4,1)S(1)} %compare_reduce_fusion.2, pred[1024]{0:T(1024)(128)(4,1)S(1)} %compare_reduce_fusion.3, pred[1024]{0:T(1024)(128)(4,1)S(1)} %compare_reduce_fusion.4, ...), kind=kLoop, calls=%fused_computation.147 | loop fusion | flops 39936 | bytes 33904 | tf_op jit(solution)/shard_map/eq | solution.py:55
  136.8 17.6 %fusion.46 = pred[1024]{0:T(1024)(128)(4,1)S(1)} fusion(pred[1024]{0:T(1024)(128)(4,1)S(1)} %compare_reduce_fusion, pred[1024]{0:T(1024)(128)(4,1)S(1)} %compare_reduce_fusion.1, pred[1024]{0:T(1024)(128)(4,1)S(1)} %compare_reduce_fusion.2, pred[1024]{0:T(1024)(128)(4,1)S(1)} %compare_reduce_fusion.3, pred[1024]{0:T(1024)(128)(4,1)S(1)} %compare_reduce_fusion.4, ...), kind=kLoop, calls=%fused_computation.144 | loop fusion | flops 37888 | bytes 33904 | tf_op jit(solution)/shard_map/eq | solution.py:55
  154.4 2.1 fusion.16
  156.4 5.1 %broadcast_in_dim.18.clone = bf16[1024,32,128]{2,0,1:T(8,128)(2,1)} broadcast(bf16[]{:T(256)} %constant.31.clone.1), dimensions={} | broadcast | bytes 8388610 | tf_op jit(solution)/shard_map/broadcast_in_dim | solution.py:127
  161.5 5.8 %scatter_fusion = bf16[1024,32,128]{2,0,1:T(8,128)(2,1)} fusion(bf16[1024,32,128]{2,0,1:T(8,128)(2,1)} %broadcast_in_dim.18.clone, s32[8]{0:T(128)S(1)} %fusion.61, bf16[8,1024,128]{2,1,0:T(8,128)(2,1)} %fusion.16), kind=kCustom, calls=%fused_computation.1 | custom fusion | bytes 6291488 | tf_op jit(solution)/shard_map/scatter | solution.py:131
  167.3 45.5 %all-to-all-done.1 = bf16[1024,32,128]{2,0,1:T(8,128)(2,1)} async-done(((bf16[1024,32,128]{2,0,1:T(8,128)(2,1)}), bf16[1024,32,128]{2,0,1:T(8,128)(2,1)}, u32[]{:S(2)}, u32[]{:S(2)}) %all-to-all-start.1) | async-done | bytes 8388640 | tf_op jit(solution)/shard_map/all_to_all | solution.py:136
  212.8 117.1 %all_to_all.15 = bf16[1024,32,128]{2,0,1:T(8,128)(2,1)} all-to-all(bf16[1024,32,128]{2,0,1:T(8,128)(2,1)} %scatter_fusion), channel_id=1, replica_groups=mesh['sky'=32,'band'=4] {'sky'}, dimensions={1} | all-to-all | bytes 16777216 | tf_op jit(solution)/shard_map/all_to_all | solution.py:137
  329.9 9.0 %convert_reduce_fusion = (f32[1024,128]{1,0:T(8,128)S(1)}, f32[1024,128]{1,0:T(8,128)S(1)}) fusion(bf16[1024,32,128]{2,0,1:T(8,128)(2,1)} %all_to_all.15, bf16[1024,32,128]{2,0,1:T(8,128)(2,1)} %all-to-all-done.1), kind=kLoop, calls=%fused_computation.3 | loop fusion | flops 20709376 | bytes 17825792 | tf_op jit(solution)/shard_map/reduce_sum | solution.py:93
  338.9 0.8 divide_convert_fusion
  341.4 3.0 copy.78
  344.5 2.8 collective-permute-done.1
  347.2 1.4 convolution_convert_fusion.1
  348.8 1.0 convolution_multiply_fusion
  349.9 4.0 all-to-all-start.2
  354.0 6.8 %all-to-all-done.2 = f32[4,256,128]{2,1,0:T(8,128)S(1)} async-done(((f32[4,256,128]{2,1,0:T(8,128)}), f32[4,256,128]{2,1,0:T(8,128)S(1)}, u32[]{:S(2)}, u32[]{:S(2)}) %all-to-all-start.2) | async-done | bytes 524320 | tf_op jit(solution)/shard_map/all_to_all | solution.py:34
  360.8 0.7 reduce_sum.29
  361.5 36.1 %all-gather.2.cloned.1.call-done = bf16[1024,4096]{1,0:T(8,128)(2,1)} async-done(((bf16[1024,128]{1,0:T(8,128)(2,1)}), bf16[1024,4096]{1,0:T(8,128)(2,1)}) %all-gather.2.cloned.1.call-update) | async-done | bytes 8388624 | tf_op jit(solution)/shard_map/all_gather | solution.py:98
  397.6 11.9 %copy.75 = bf16[1024,4096]{0,1:T(8,128)(2,1)} copy(bf16[1024,4096]{1,0:T(8,128)(2,1)} %all-gather.2.cloned.1.call-done) | data formatting | bytes 16777216 | tf_op jit(solution)/shard_map/all_gather | solution.py:98
  409.5 11.9 %copy.76 = bf16[1024,32,128]{2,0,1:T(8,128)(2,1)} copy(bf16[1024,32,128]{0,2,1:T(8,128)(2,1)} %bitcast.239) | data formatting | bytes 16777216 | tf_op jit(solution)/shard_map/reshape | solution.py:98
  421.4 5.5 %gather_fusion = bf16[8,1024,128]{2,1,0:T(8,128)(2,1)} fusion(bf16[1024,32,128]{2,0,1:T(8,128)(2,1)} %copy.76, s32[1024]{0:T(1024)S(1)} %pad_clamp_fusion), kind=kCustom, calls=%fused_computation | custom fusion | bytes 4194336 | tf_op jit(solution)/shard_map/jit(_take)/gather | solution.py:101
  426.9 2.9 copy.77
  429.8 4.1 subtract_convert_fusion
  433.9 3.9 copy.79
  (78 shorter events, 5.4 us)
Async XLA Ops:
  7.2 76.4 %copy-start = (s32[32,4,8]{0,2,1:T(8,128)S(1)}, s32[32,4,8]{0,2,1:T(8,128)}, u32[]{:S(2)}) copy-start(s32[32,4,8]{0,2,1:T(8,128)} %param.11) | copy-start | bytes 12292
  10.3 0.7 copy-start.5
  10.3 0.7 copy-start.6
  45.4 8.2 %copy-start.2 = (bf16[9,1024,1024]{2,1,0:T(8,128)(2,1)S(1)}, bf16[9,1024,1024]{2,1,0:T(8,128)(2,1)}, u32[]{:S(2)}) copy-start(bf16[9,1024,1024]{2,1,0:T(8,128)(2,1)} %copy.65) | copy-start | bytes 56623108
  68.4 2.4 copy-start.7
  94.6 118.2 %all-to-all-start.1 = ((bf16[1024,32,128]{2,0,1:T(8,128)(2,1)}), bf16[1024,32,128]{2,0,1:T(8,128)(2,1)}, u32[]{:S(2)}, u32[]{:S(2)}) async-start(bf16[1024,32,128]{2,0,1:T(8,128)(2,1)} %scatter_fusion.1), calls=%async_computation.1 | async-start | bytes 16777216 | tf_op jit(solution)/shard_map/all_to_all | solution.py:136
  104.2 3.4 copy-start.4
  104.3 293.3 %all-gather.2.cloned.1.call-start = ((), (), s32[]{:S(2)}) async-start(), calls=%async_computation.3 | async-start | bytes 8650752 | tf_op jit(solution)/shard_map/all_gather | solution.py:98
  329.9 10.2 %copy-start.8 = (f32[1,31]{1,0:T(1,128)S(1)}, f32[1,31]{1,0:T(1,128)}, u32[]{:S(2)}) copy-start(f32[1,31]{1,0:T(1,128)} %param.15) | copy-start | bytes 376
  339.7 0.9 copy-start.3
  340.8 3.7 collective-permute-start
  341.1 6.1 %collective-permute-start.1 = (bf16[1024,15]{1,0:T(8,128)(2,1)S(1)}, bf16[1024,15]{1,0:T(8,128)(2,1)}, u32[]{:S(2)}, u32[]{:S(2)}) collective-permute-start(bf16[1024,15]{1,0:T(8,128)(2,1)S(1)} %get-tuple-element.11), channel_id=1, source_target_pairs={{4,0},{8,4},{12,8},{16,12},{20,16},{24,20},{28,24},{32,28},{36,32}... | collective-permute-start | bytes 92168 | tf_op jit(solution)/shard_map/ppermute | solution.py:21
  349.9 11.0 %all-to-all-start.2 = ((f32[4,256,128]{2,1,0:T(8,128)}), f32[4,256,128]{2,1,0:T(8,128)S(1)}, u32[]{:S(2)}, u32[]{:S(2)}) async-start(f32[4,256,128]{2,1,0:T(8,128)} %bitcast.124), calls=%async_computation.2 | async-start | bytes 1048576 | tf_op jit(solution)/shard_map/all_to_all | solution.py:34
  429.8 8.1 %copy-start.1 = (s32[32,4,8]{0,2,1:T(8,128)S(1)}, s32[32,4,8]{0,2,1:T(8,128)}, u32[]{:S(2)}) copy-start(s32[32,4,8]{0,2,1:T(8,128)} %param.11) | copy-start | bytes 12292
Sparse Core Ops, SparseCore 0:
  339.9 57.6 all-gather.1
where the time goes:
time: 447 us; the launch traced here: 445 us
  local copies, waits for them, and re-layouts  123 us (28%)
  blocking collectives  117 us (26%)
  waiting for transfers between devices  91.2 us (20%)
  other arithmetic  61.9 us (14%)
  matrix products  23.2 us (5%)
  starting transfers between devices  14.3 us (3%)
  between operations  14.3 us (3%)
    all_to_all x1, blocking collectives, body(): lax.all_to_all(send_weight, 'sky', split_axis=1, concat_axis=1, tiled=True)  117 us
    all_to_all x1, waiting for transfers between devices, body(): lax.all_to_all(send_matched, 'sky', split_axis=1, concat_axis=1, tiled=True)  45.5 us
    all_gather x1, waiting for transfers between devices, subtract_template(): lax.all_gather(template, 'sky', axis=1, tiled=True)  36.1 us
    eq x2, other arithmetic, keep_pixels(): return jnp.logical_and(row_bits[:, None] == 0, column_bits[None, :] == 0)  34.9 us
    unnamed x43, local copies, waits for them, and re-layouts  33.6 us
    convert_element_type x1, local copies, waits for them, and re-layouts, psf_match(): column_pass.reshape(NB, side_length, side_length).astype(jnp.bfloat16)  24.6 us
    all_gather x1, local copies, waits for them, and re-layouts, subtract_template(): lax.all_gather(template, 'sky', axis=1, tiled=True)  11.9 us
    reshape x1, local copies, waits for them, and re-layouts, subtract_template(): lax.all_gather(template, 'sky', axis=1, tiled=True)  11.9 us
  transfers between devices with their start and end apart: 5, of which 5 were waited for; matrix products, arithmetic and copies ran while one was open for 16% of the time, Pallas kernels for 0%

commit v1 on v0

--- a/solution.py
+++ b/solution.py
@@ -134,7 +134,12 @@
     template = average_pieces(
         (
             lax.all_to_all(send_matched, "sky", split_axis=1, concat_axis=1, tiled=True),
-            lax.all_to_all(send_weight, "sky", split_axis=1, concat_axis=1, tiled=True),
+            jnp.concatenate(
+                lax.all_to_all(
+                    jnp.stack(jnp.split(send_weight, lax.axis_size("sky"), axis=1)), "sky", 0, 0
+                ),
+                axis=1,
+            ),
         )
     )
     difference = subtract_template(template, matched, own_columns, side_length, sky_count)

time: 447 us -> 511 us (1.14)
  blocking collectives: 117 us -> 0 us
  waiting for transfers between devices: 91.2 us -> 170 us
  local copies, waits for them, and re-layouts: 123 us -> 181 us
  starting transfers between devices: 14.3 us -> 53.9 us
    all_to_all x1 -> x0, blocking collectives: 117 us -> none  [body(): lax.all_to_all(send_weight, 'sky', split_axis=1, concat_axis=1, tiled=True)]
    all_to_all x1, waiting for transfers between devices: 45.5 us -> 104 us  [body(): lax.all_to_all(send_matched, 'sky', split_axis=1, concat_axis=1, tiled=True)]
    unnamed x43 -> x72, local copies, waits for them, and re-layouts: 33.6 us -> 85 us
    all_to_all x0 -> x1, waiting for transfers between devices: none -> 20.4 us  [body(): lax.all_to_all(jnp.stack(jnp.split(send_weight, lax.axis_size('sky'), axi...]
    all_to_all x1, starting transfers between devices: 9.63 us -> 22.7 us  [body(): lax.all_to_all(send_matched, 'sky', split_axis=1, concat_axis=1, tiled=True)]
    ppermute x1, starting transfers between devices: 0.34 us -> 12 us  [with_halo(): lax.ppermute(lax.slice_in_dim(block, block.shape[dim] - width, None, axis...]
    all_to_all x0 -> x1, starting transfers between devices: none -> 9.62 us  [body(): lax.all_to_all(jnp.stack(jnp.split(send_weight, lax.axis_size('sky'), axi...]
    reduce_sum x0 -> x1, other arithmetic: none -> 8.45 us  [average_pieces(): numer = jnp.sum(weight_float * matched_in.astype(jnp.float32), axis=1)]
  transfers between devices with their start and end apart: 5 -> 6, of which waited for: 5 -> 5; matrix products, arithmetic and copies ran while one was open for 16% -> 19% of each run, Pallas kernels for 0% -> 0%
where the time goes in v1:
time: 511 us; the launch traced here: 507 us
  local copies, waits for them, and re-layouts  181 us (35%)
  waiting for transfers between devices  170 us (33%)
  other arithmetic  64.7 us (13%)
  starting transfers between devices  53.9 us (11%)
  matrix products  22.3 us (4%)
  between operations  14.4 us (3%)
    all_to_all x1, waiting for transfers between devices, body(): lax.all_to_all(send_matched, 'sky', split_axis=1, concat_axis=1, tiled=True)  104 us
    unnamed x72, local copies, waits for them, and re-layouts  85 us
    all_gather x1, waiting for transfers between devices, subtract_template(): lax.all_gather(template, 'sky', axis=1, tiled=True)  38.4 us
    eq x2, other arithmetic, keep_pixels(): return jnp.logical_and(row_bits[:, None] == 0, column_bits[None, :] == 0)  34.9 us
    convert_element_type x1, local copies, waits for them, and re-layouts, psf_match(): column_pass.reshape(NB, side_length, side_length).astype(jnp.bfloat16)  24.6 us
    all_to_all x1, starting transfers between devices, body(): lax.all_to_all(send_matched, 'sky', split_axis=1, concat_axis=1, tiled=True)  22.7 us
    all_to_all x1, waiting for transfers between devices, body(): lax.all_to_all(jnp.stack(jnp.split(send_weight, lax.axis_size('sky'), axi...  20.4 us
    ppermute x1, starting transfers between devices, with_halo(): lax.ppermute(lax.slice_in_dim(block, block.shape[dim] - width, None, axis...  12 us
  transfers between devices with their start and end apart: 6, of which 5 were waited for; matrix products, arithmetic and copies ran while one was open for 19% of the time, Pallas kernels for 0%

profile of v1, /device:TPU:1, one launch (start us, length us, event | category | flops | bytes accessed | tf_op | source)
XLA Modules:
  0.0 507.0 jit_solution(10853572131441409011)
XLA Ops:
  8.3 2.1 fusion.98
  10.4 1.9 fusion.101
  12.3 2.1 fusion.99
  14.4 2.1 fusion.100
  16.7 2.2 copy.86
  18.9 4.5 compare_select_fusion.2
  23.4 4.3 compare_select_fusion.1
  27.8 17.4 %fusion.83 = pred[8,128]{1,0:T(8,128)(4,1)S(1)} fusion(pred[1024]{0:T(1024)(128)(4,1)S(1)} %compare_reduce_fusion, pred[1024]{0:T(1024)(128)(4,1)S(1)} %compare_reduce_fusion.1, pred[1024]{0:T(1024)(128)(4,1)S(1)} %compare_reduce_fusion.2, pred[1024]{0:T(1024)(128)(4,1)S(1)} %compare_reduce_fusion.3, pred[1024]{0:T(1024)(128)(4,1)S(1)} %compare_reduce_fusion.4, ...), kind=kLoop, calls=%fused_computation.213 | loop fusion | flops 39936 | bytes 33904 | tf_op jit(solution)/shard_map/eq | solution.py:55
  45.2 17.5 %fusion.80 = pred[1024]{0:T(1024)(128)(4,1)S(1)} fusion(pred[1024]{0:T(1024)(128)(4,1)S(1)} %compare_reduce_fusion, pred[1024]{0:T(1024)(128)(4,1)S(1)} %compare_reduce_fusion.1, pred[1024]{0:T(1024)(128)(4,1)S(1)} %compare_reduce_fusion.2, pred[1024]{0:T(1024)(128)(4,1)S(1)} %compare_reduce_fusion.3, pred[1024]{0:T(1024)(128)(4,1)S(1)} %compare_reduce_fusion.4, ...), kind=kLoop, calls=%fused_computation.210 | loop fusion | flops 37888 | bytes 33904 | tf_op jit(solution)/shard_map/eq | solution.py:55
  63.4 5.1 %broadcast_in_dim.18.clone = bf16[1024,32,128]{2,0,1:T(8,128)(2,1)} broadcast(bf16[]{:T(256)} %constant.31.clone.1), dimensions={} | broadcast | bytes 8388610 | tf_op jit(solution)/shard_map/broadcast_in_dim | solution.py:127
  68.5 5.1 scatter_fusion
  73.6 1.7 fusion.74
  93.6 1.7 fusion.62
  98.6 1.7 fusion.59
  118.6 1.7 fusion.47
  127.0 9.6 %all-to-all-start = ((bf16[32,1024,1,128]{3,1,2,0:T(8,128)(2,1)}), bf16[32,1024,1,128]{3,1,2,0:T(8,128)(2,1)}, u32[]{:S(2)}, u32[]{:S(2)}) async-start(bf16[32,1024,1,128]{3,1,2,0:T(8,128)(2,1)} %fusion.43), calls=%async_computation | async-start | bytes 16777216 | tf_op jit(solution)/shard_map/all_to_all | solution.py:138
  136.6 2.9 copy.63
  140.8 9.2 %convolution_convert_fusion = bf16[9,128,8,1024]{3,1,2,0:T(8,128)(2,1)} fusion(bf16[8,1024,152]{1,2,0:T(8,128)(2,1)S(1)} %fusion.36, bf16[9,152,128,1]{2,0,1,3:T(8,128)(2,1)S(1)} %fusion.21), kind=kOutput, calls=%fused_computation.10 | convolution fusion | flops 2878341120 | bytes 21714944 | tf_op jit(solution)/shard_map/jyw,kwt->kyjt/dot_general | solution.py:72
  150.0 24.6 %copy.65 = bf16[9,1024,1024]{2,1,0:T(8,128)(2,1)} copy(bf16[9,1024,1024]{1,2,0:T(8,128)(2,1)} %bitcast.377) | data formatting | bytes 37748736 | tf_op jit(solution)/shard_map/convert_element_type | solution.py:75
  174.6 4.3 fusion.4
  179.0 3.8 copy-done.2
  182.8 2.5 fusion.12
  185.2 2.4 fusion.11
  187.7 2.5 fusion.10
  190.2 2.5 fusion.9
  192.7 2.4 fusion.8
  195.1 2.4 fusion.7
  197.5 2.4 fusion.6
  200.6 9.9 %bitcast_convert_fusion = bf16[128,8,1024]{2,0,1:T(8,128)(2,1)S(1)} fusion(bf16[8,9,152,1024]{3,2,1,0:T(8,128)(2,1)} %fusion.6, bf16[9,152,128]{2,0,1:T(8,128)(2,1)S(1)} %fusion.22), kind=kOutput, calls=%fused_computation.11 | convolution fusion | flops 2869952512 | bytes 24860672 | tf_op jit(solution)/shard_map/ikwx,kwt->itx/dot_general | solution.py:85
  212.8 5.1 %broadcast_in_dim.18.clone.1 = bf16[1024,32,128]{2,0,1:T(8,128)(2,1)} broadcast(bf16[]{:T(256)} %constant.31.clone.1), dimensions={} | broadcast | bytes 8388610 | tf_op jit(solution)/shard_map/broadcast_in_dim | solution.py:127
  217.9 5.7 %scatter_fusion.1 = bf16[1024,32,128]{2,0,1:T(8,128)(2,1)} fusion(bf16[1024,32,128]{2,0,1:T(8,128)(2,1)} %broadcast_in_dim.18.clone.1, s32[8]{0:T(128)S(1)} %fusion.95, bf16[8,1024,128]{2,1,0:T(8,128)(2,1)} %bitcast.389), kind=kCustom, calls=%fused_computation.2 | custom fusion | bytes 6291488 | tf_op jit(solution)/shard_map/scatter | solution.py:128
  223.6 20.4 %all-to-all-done = bf16[32,1024,1,128]{3,1,2,0:T(8,128)(2,1)} async-done(((bf16[32,1024,1,128]{3,1,2,0:T(8,128)(2,1)}), bf16[32,1024,1,128]{3,1,2,0:T(8,128)(2,1)}, u32[]{:S(2)}, u32[]{:S(2)}) %all-to-all-start) | async-done | bytes 8388640 | tf_op jit(solution)/shard_map/all_to_all | solution.py:138
  244.1 22.7 %all-to-all-start.1 = ((bf16[1024,32,128]{2,0,1:T(8,128)(2,1)}), bf16[1024,32,128]{2,0,1:T(8,128)(2,1)}, u32[]{:S(2)}, u32[]{:S(2)}) async-start(bf16[1024,32,128]{2,0,1:T(8,128)(2,1)} %scatter_fusion.1), calls=%async_computation.1 | async-start | bytes 16777216 | tf_op jit(solution)/shard_map/all_to_all | solution.py:136
  266.8 4.7 fusion
  271.5 103.7 %all-to-all-done.1 = bf16[1024,32,128]{2,0,1:T(8,128)(2,1)} async-done(((bf16[1024,32,128]{2,0,1:T(8,128)(2,1)}), bf16[1024,32,128]{2,0,1:T(8,128)(2,1)}, u32[]{:S(2)}, u32[]{:S(2)}) %all-to-all-start.1) | async-done | bytes 8388640 | tf_op jit(solution)/shard_map/all_to_all | solution.py:136
  375.3 8.4 %fusion.2 = f32[1024,128]{1,0:T(8,128)S(1)} fusion(bf16[32,1024,1,128]{3,1,2,0:T(8,128)(2,1)} %all-to-all-done, bf16[1024,32,128]{2,0,1:T(8,128)(2,1)} %all-to-all-done.1), kind=kLoop, calls=%fused_computation.9 | loop fusion | flops 16646144 | bytes 17301504 | tf_op jit(solution)/shard_map/reduce_sum | solution.py:92
  386.6 5.5 %collective-permute-start.1 = (bf16[1024,15]{1,0:T(8,128)(2,1)S(1)}, bf16[1024,15]{1,0:T(8,128)(2,1)S(1)}, u32[]{:S(2)}, u32[]{:S(2)}) collective-permute-start(bf16[1024,15]{1,0:T(8,128)(2,1)S(1)} %get-tuple-element.9), channel_id=1, source_target_pairs={{4,0},{8,4},{12,8},{16,12},{20,16},{24,20},{28,24},{32,28},{36,32}... | collective-permute-start | bytes 92168 | tf_op jit(solution)/shard_map/ppermute | solution.py:21
  392.2 12.0 %collective-permute-start = (bf16[1024,15]{1,0:T(8,128)(2,1)S(1)}, bf16[1024,15]{1,0:T(8,128)(2,1)S(1)}, u32[]{:S(2)}, u32[]{:S(2)}) collective-permute-start(bf16[1024,15]{1,0:T(8,128)(2,1)S(1)} %get-tuple-element.8), channel_id=1, source_target_pairs={{0,4},{4,8},{8,12},{12,16},{16,20},{20,24},{24,28},{28,32},{32,36}... | collective-permute-start | bytes 92168 | tf_op jit(solution)/shard_map/ppermute | solution.py:18
  404.2 3.0 copy.78
  409.8 4.1 all-to-all-start.2
  414.0 6.9 %all-to-all-done.2 = f32[4,256,128]{2,1,0:T(8,128)S(1)} async-done(((f32[4,256,128]{2,1,0:T(8,128)}), f32[4,256,128]{2,1,0:T(8,128)S(1)}, u32[]{:S(2)}, u32[]{:S(2)}) %all-to-all-start.2) | async-done | bytes 524320 | tf_op jit(solution)/shard_map/all_to_all | solution.py:34
  421.5 38.4 %all-gather.2.cloned.1.call-done = bf16[1024,4096]{1,0:T(8,128)(2,1)} async-done(((bf16[1024,128]{1,0:T(8,128)(2,1)}), bf16[1024,4096]{1,0:T(8,128)(2,1)}) %all-gather.2.cloned.1.call-update) | async-done | bytes 8388624 | tf_op jit(solution)/shard_map/all_gather | solution.py:98
  459.9 11.9 %copy.75 = bf16[1024,4096]{0,1:T(8,128)(2,1)} copy(bf16[1024,4096]{1,0:T(8,128)(2,1)} %all-gather.2.cloned.1.call-done) | data formatting | bytes 16777216 | tf_op jit(solution)/shard_map/all_gather | solution.py:98
  471.9 11.9 %copy.76 = bf16[1024,32,128]{2,0,1:T(8,128)(2,1)} copy(bf16[1024,32,128]{0,2,1:T(8,128)(2,1)} %bitcast.378) | data formatting | bytes 16777216 | tf_op jit(solution)/shard_map/reshape | solution.py:98
  483.8 5.5 %gather_fusion = bf16[8,1024,128]{2,1,0:T(8,128)(2,1)} fusion(bf16[1024,32,128]{2,0,1:T(8,128)(2,1)} %copy.76, s32[1024]{0:T(1024)S(1)} %pad_clamp_fusion), kind=kCustom, calls=%fused_computation | custom fusion | bytes 4194336 | tf_op jit(solution)/shard_map/jit(_take)/gather | solution.py:101
  489.3 2.9 copy.77
  492.2 4.1 subtract_convert_fusion
  496.3 3.9 copy.79
  (110 shorter events, 59.1 us)
Async XLA Ops:
  7.2 9.3 %copy-start = (s32[32,4,8]{0,2,1:T(8,128)S(1)}, s32[32,4,8]{0,2,1:T(8,128)}, u32[]{:S(2)}) copy-start(s32[32,4,8]{0,2,1:T(8,128)} %param.11) | copy-start | bytes 12292
  127.0 117.1 %all-to-all-start = ((bf16[32,1024,1,128]{3,1,2,0:T(8,128)(2,1)}), bf16[32,1024,1,128]{3,1,2,0:T(8,128)(2,1)}, u32[]{:S(2)}, u32[]{:S(2)}) async-start(bf16[32,1024,1,128]{3,1,2,0:T(8,128)(2,1)} %fusion.43), calls=%async_computation | async-start | bytes 16777216 | tf_op jit(solution)/shard_map/all_to_all | solution.py:138
  136.6 3.6 copy-start.4
  136.6 3.6 copy-start.5
  174.6 8.2 %copy-start.2 = (bf16[9,1024,1024]{2,1,0:T(8,128)(2,1)S(1)}, bf16[9,1024,1024]{2,1,0:T(8,128)(2,1)}, u32[]{:S(2)}) copy-start(bf16[9,1024,1024]{2,1,0:T(8,128)(2,1)} %copy.65) | copy-start | bytes 56623108
  197.5 2.4 copy-start.6
  244.1 131.2 %all-to-all-start.1 = ((bf16[1024,32,128]{2,0,1:T(8,128)(2,1)}), bf16[1024,32,128]{2,0,1:T(8,128)(2,1)}, u32[]{:S(2)}, u32[]{:S(2)}) async-start(bf16[1024,32,128]{2,0,1:T(8,128)(2,1)} %scatter_fusion.1), calls=%async_computation.1 | async-start | bytes 16777216 | tf_op jit(solution)/shard_map/all_to_all | solution.py:136
  266.8 193.2 %all-gather.2.cloned.1.call-start = ((), (), s32[]{:S(2)}) async-start(), calls=%async_computation.3 | async-start | bytes 8650752 | tf_op jit(solution)/shard_map/all_gather | solution.py:98
  271.5 113.4 %copy-start.7 = (f32[1,31]{1,0:T(1,128)S(1)}, f32[1,31]{1,0:T(1,128)}, u32[]{:S(2)}) copy-start(f32[1,31]{1,0:T(1,128)} %param.15) | copy-start | bytes 376
  384.5 23.6 %copy-start.3 = (bf16[1024,128]{1,0:T(8,128)(2,1)S(1)}, bf16[1024,128]{1,0:T(8,128)(2,1)}, u32[]{:S(2)}) copy-start(bf16[1024,128]{1,0:T(8,128)(2,1)} %divide_convert_fusion) | copy-start | bytes 786436
  386.6 21.5 %collective-permute-start.1 = (bf16[1024,15]{1,0:T(8,128)(2,1)S(1)}, bf16[1024,15]{1,0:T(8,128)(2,1)S(1)}, u32[]{:S(2)}, u32[]{:S(2)}) collective-permute-start(bf16[1024,15]{1,0:T(8,128)(2,1)S(1)} %get-tuple-element.9), channel_id=1, source_target_pairs={{4,0},{8,4},{12,8},{16,12},{20,16},{24,20},{28,24},{32,28},{36,32}... | collective-permute-start | bytes 92168 | tf_op jit(solution)/shard_map/ppermute | solution.py:21
  392.2 15.9 %collective-permute-start = (bf16[1024,15]{1,0:T(8,128)(2,1)S(1)}, bf16[1024,15]{1,0:T(8,128)(2,1)S(1)}, u32[]{:S(2)}, u32[]{:S(2)}) collective-permute-start(bf16[1024,15]{1,0:T(8,128)(2,1)S(1)} %get-tuple-element.8), channel_id=1, source_target_pairs={{0,4},{4,8},{8,12},{12,16},{16,20},{20,24},{24,28},{28,32},{32,36}... | collective-permute-start | bytes 92168 | tf_op jit(solution)/shard_map/ppermute | solution.py:18
  409.8 11.0 %all-to-all-start.2 = ((f32[4,256,128]{2,1,0:T(8,128)}), f32[4,256,128]{2,1,0:T(8,128)S(1)}, u32[]{:S(2)}, u32[]{:S(2)}) async-start(f32[4,256,128]{2,1,0:T(8,128)} %bitcast.158), calls=%async_computation.2 | async-start | bytes 1048576 | tf_op jit(solution)/shard_map/all_to_all | solution.py:34
  489.3 10.9 %copy-start.1 = (s32[32,4,8]{0,2,1:T(8,128)S(1)}, s32[32,4,8]{0,2,1:T(8,128)}, u32[]{:S(2)}) copy-start(s32[32,4,8]{0,2,1:T(8,128)} %param.11) | copy-start | bytes 12292
Sparse Core Ops, SparseCore 0:
  384.7 75.1 all-gather.1
